TPU v7x, 32 devices: a whole 2x2x4 slice. The times are simulated.
32 devices in a mesh: parts: 2 (over y), tile: 4 (over x, core), chan: 4 (over z).
Axes of the slice: x: 2, y: 2, z: 4, core: 2. Of those that a mesh axis runs over, the one named last changes fastest.
Arguments:
- weather: bfloat16 [768, 64, 1440], P('chan', 'parts', 'tile'), parts along dimension 1, may hold values from -6 to 6
- lon_taps: float32 [9, 768], P(None, 'chan'), may hold values from -4 to 4
- latitude_taps: float32 [9, 768], P(None, 'chan'), may hold values from -2 to 2
- norm_gain: float32 [768], replicated, may hold values from 0.1 to 1.9
- up_weight: bfloat16 [768, 3072], P(None, ('tile', 'chan')), may hold values from -0.21875 to 0.21875
- down_weight: bfloat16 [768, 3072], P(None, ('tile', 'chan')), may hold values from -0.109375 to 0.109375
Outputs:
- mixed: bfloat16 [768, 64, 1440], P('chan', 'parts', 'tile'), parts along dimension 1
There are 2 independent parts, one for each index of `parts`. A program takes and returns all parts, laid end to end along the dimension named above; an argument that names none is the same for every part. Nothing has to cross between parts.
All inputs are finite; a program needn't handle non-finite values.
Results may differ from a plain program's by a relative error of at most 0.0065.
Values may be sent and summed in bfloat16 or wider, within the bound.
No kernel may reach another device: no remote copies, remote signals or barrier semaphores. Data moves between devices by JAX's collectives and lax.ppermute only.
A program may use at most 128 MiB of HBM per device.

v0:
```python
import jax
import jax.numpy as jnp
from jax import lax
from jax.sharding import PartitionSpec as P

KERNEL_TAPS = 9
DILATION_STEP = 2


def with_halo(shard, sides, width):
    for axis, dim in sides:
        devices, length = (lax.axis_size(axis), shard.shape[dim])
        up = [(i, (i + 1) % devices) for i in range(devices)]
        down = [(j, i) for i, j in up]
        last = lax.slice_in_dim(shard, length - width, length, axis=dim)
        initial = lax.slice_in_dim(shard, 0, width, axis=dim)
        before = lax.ppermute(last, axis, up)
        after = lax.ppermute(initial, axis, down)
        shard = jnp.concatenate([before, shard, after], axis=dim)
    return shard


def layer_norm(values, norm_gain):
    as_float = values.astype(jnp.float32)
    center = jnp.mean(as_float, axis=0)
    deviation = as_float - center
    spread_sq = jnp.mean(deviation * deviation, axis=0)
    return (deviation * lax.rsqrt(spread_sq + 1e-06) * norm_gain[:, None]).astype(jnp.bfloat16)


def on_device(weather, lon_taps, latitude_taps, norm_gain, up_weight, down_weight):
    chan_count, row_total, column_total = weather.shape
    border_width = DILATION_STEP * (KERNEL_TAPS // 2)
    widened_field = with_halo(weather, (("tile", 2),), border_width)
    lon_sum = jnp.zeros(weather.shape, jnp.float32)
    for kernel_tap_index in range(KERNEL_TAPS):
        sliding_window = widened_field[
            :, :, DILATION_STEP * kernel_tap_index : DILATION_STEP * kernel_tap_index + column_total
        ].astype(jnp.float32)
        lon_sum = lon_sum + lon_taps[kernel_tap_index][:, None, None] * sliding_window
    padded_field = jnp.pad(lon_sum, ((0, 0), (border_width, border_width), (0, 0)))
    latitude_sum = jnp.zeros(weather.shape, jnp.float32)
    for kernel_tap_index in range(KERNEL_TAPS):
        latitude_sum = (
            latitude_sum
            + latitude_taps[kernel_tap_index][:, None, None]
            * padded_field[
                :,
                DILATION_STEP * kernel_tap_index : DILATION_STEP * kernel_tap_index + row_total,
                :,
            ]
        )
    spatial = latitude_sum.astype(jnp.bfloat16)
    group_count = lax.axis_size("chan")
    width_all = chan_count * group_count
    shard_width = up_weight.shape[1]
    by_cell = lax.all_to_all(spatial, "chan", split_axis=1, concat_axis=0, tiled=True)
    cell_count = by_cell.shape[1] * by_cell.shape[2]
    normed = layer_norm(by_cell.reshape(width_all, cell_count), norm_gain)
    expanded = lax.dot_general(
        lax.all_gather(up_weight, ("tile", "chan"), axis=1, tiled=True),
        normed,
        (((0,), (0,)), ((), ())),
        preferred_element_type=jnp.float32,
    )
    hidden = jax.nn.gelu(expanded, approximate=False).astype(jnp.bfloat16)
    down_all = lax.all_gather(down_weight, ("tile", "chan"), axis=1, tiled=True)
    tile_count = down_all.shape[1] // (group_count * shard_width)
    down_groups = down_all.reshape(width_all, tile_count, group_count, shard_width)
    hidden_groups = hidden.reshape(tile_count, group_count, shard_width, cell_count)
    summed = jnp.zeros((width_all, cell_count), jnp.float32)
    for group in range(group_count):
        group_value = jnp.einsum(
            "dts,tsc->dc",
            down_groups[:, :, group, :],
            hidden_groups[:, group],
            preferred_element_type=jnp.float32,
        ).astype(jnp.bfloat16)
        group_value = lax.optimization_barrier(group_value)
        summed = summed + group_value.astype(jnp.float32)
    update_cells = summed.astype(jnp.bfloat16).reshape(width_all, by_cell.shape[1], column_total)
    update = lax.all_to_all(update_cells, "chan", split_axis=0, concat_axis=1, tiled=True)
    return (weather.astype(jnp.float32) + update.astype(jnp.float32)).astype(jnp.bfloat16)


def solution(mesh):
    return jax.shard_map(
        on_device,
        mesh=mesh,
        in_specs=(
            P("chan", "parts", "tile"),
            P(None, "chan"),
            P(None, "chan"),
            P(),
            P(None, ("tile", "chan")),
            P(None, ("tile", "chan")),
        ),
        out_specs=P("chan", "parts", "tile"),
        check_vma=False,
    )
```

profile of v0, /device:TPU:0, one launch (start us, length us, event | category | flops | bytes accessed | tf_op | source)
XLA Modules:
  0.0 563.3 jit_solution(12894988400171444290)
XLA Ops:
  7.3 2.6 fusion.56
  11.2 2.4 collective-permute-start.1
  15.0 4.3 collective-permute-done
  22.0 36.4 %fusion.22 = f32[192,32,360]{2,1,0:T(8,128)} fusion(bf16[192,32,360]{2,1,0:T(8,128)(2,1)} %param.6, bf16[192,32,8]{2,1,0:T(8,128)(2,1)S(1)} %copy.38, bf16[192,32,8]{2,1,0:T(8,128)(2,1)S(1)} %copy.36, f32[192]{0:T(256)S(1)} %bitcast.205, f32[192]{0:T(256)S(1)} %bitcast.206, f32[192]{0:T(256)S(1)} %bitcast.199, f32[192]{0:T(256)S(1)} %bitcast.200, ...), kind=kLoop, calls=%fused_computation.38 | loop fusion | flops 110592000 | bytes 13474560 | tf_op jit(solution)/shard_map/add | solution.py:40
  58.4 34.3 %fusion.33 = bf16[192,32,360]{2,1,0:T(8,128)(2,1)S(1)} fusion(f32[192,32,360]{2,1,0:T(8,128)} %fusion.22, f32[192]{0:T(256)S(1)} %bitcast.196, f32[192]{0:T(256)S(1)} %bitcast.197, f32[192]{0:T(256)S(1)} %bitcast.190, f32[192]{0:T(256)S(1)} %bitcast.191, f32[192]{0:T(256)S(1)} %bitcast.192, f32[192]{0:T(256)S(1)} %bitcast.193, f32[192]{0:T(256)S(1)} %bitcast.194, ...), kind=kLoop, calls=%fused_computation.49 | loop fusion | flops 39813120 | bytes 13277952 | tf_op jit(solution)/shard_map/convert_element_type | solution.py:53
  92.7 4.0 copy.39
  96.7 5.0 all-to-all-start
  102.4 130.9 %all-to-all-done = bf16[192,32,360]{2,0,1:T(8,128)(2,1)} async-done(((bf16[192,32,360]{2,0,1:T(8,128)(2,1)}), bf16[192,32,360]{2,0,1:T(8,128)(2,1)}, u32[]{:S(2)}, u32[]{:S(2)}) %all-to-all-start) | async-done | bytes 4423712 | tf_op jit(solution)/shard_map/all_to_all | solution.py:57
  233.2 3.5 bitcast_convert_fusion.4
  236.7 5.0 fusion.55
  241.7 9.1 %copy.68 = f32[192,4,8,360]{3,2,0,1:T(8,128)} copy(f32[192,4,8,360]{3,0,2,1:T(8,128)S(1)} %bitcast_convert_fusion.4) | data formatting | bytes 17694720 | tf_op jit(solution)/shard_map/convert_element_type | solution.py:24
  250.8 5.0 multiply_reduce_fusion
  255.9 11.5 %reshape.71 = f32[768,2880]{1,0:T(8,128)} reshape(f32[4,192,8,360]{3,2,1,0:T(8,128)} %bitcast.180) | data formatting | bytes 17694720 | tf_op jit(solution)/shard_map/convert_element_type | solution.py:24
  267.5 7.2 %multiply_convert_fusion.1.clone.4 = bf16[768,2880]{1,0:T(8,128)(2,1)} fusion(f32[768,2880]{1,0:T(8,128)} %reshape.71, f32[768]{0:T(1024)S(1)} %copy-done.3, f32[2880]{0:T(1024)S(1)} %rsqrt.11, f32[2880]{0:T(1024)S(1)} %div.9), kind=kLoop, calls=%fused_computation.60.clone.clone.clone.clone.1 | loop fusion | flops 8847360 | bytes 13297152 | tf_op jit(solution)/shard_map/convert_element_type | solution.py:66
  274.7 102.8 %fusion.2 = bf16[3072,2880]{0,1:T(8,128)(2,1)} fusion(bf16[768,3072]{0,1:T(8,128)(2,1)} %all-gather.3.cloned.1.call-done, bf16[768,2880]{1,0:T(8,128)(2,1)} %multiply_convert_fusion.1.clone.4), kind=kOutput, calls=%fused_computation.3 | convolution fusion | flops 14164623360 | bytes 26836992 | tf_op jit(solution)/shard_map/dot_general | solution.py:60
  377.5 22.1 %copy.41 = bf16[3072,2880]{1,0:T(8,128)(2,1)} copy(bf16[3072,2880]{0,1:T(8,128)(2,1)} %fusion.2) | data formatting | bytes 35389440 | tf_op jit(solution)/shard_map/convert_element_type | solution.py:66
  399.7 8.7 %fusion.53 = bf16[768,2880]{0,1:T(8,128)(2,1)} fusion(bf16[4,4,192,2880]{3,2,1,0:T(8,128)(2,1)} %bitcast.184, bf16[768,4,4,192]{0,3,2,1:T(8,128)(2,1)} %bitcast.207), kind=kOutput, calls=%fused_computation.92 | convolution fusion | flops 3399598080 | bytes 10125312 | tf_op jit(solution)/shard_map/dts,tsc->dc/dot_general | solution.py:73
  410.5 5.5 fusion.52
  415.9 5.6 fusion.51
  421.5 5.7 %fusion.54 = bf16[768,2880]{0,1:T(8,128)(2,1)} fusion(bf16[4,4,192,2880]{3,2,1,0:T(8,128)(2,1)S(1)} %bitcast.187, bf16[768,4,4,192]{0,3,2,1:T(8,128)(2,1)S(1)} %bitcast.210), kind=kOutput, calls=%fused_computation.93 | convolution fusion | flops 3399598080 | bytes 10125312 | tf_op jit(solution)/shard_map/dts,tsc->dc/dot_general | solution.py:73
  427.2 10.3 %add_convert_fusion = bf16[768,2880]{0,1:T(8,128)(2,1)} fusion(bf16[768,2880]{0,1:T(8,128)(2,1)} %fusion.54, bf16[768,2880]{0,1:T(8,128)(2,1)} %fusion.53, bf16[768,2880]{0,1:T(8,128)(2,1)} %fusion.52, bf16[768,2880]{0,1:T(8,128)(2,1)} %fusion.51), kind=kLoop, calls=%fused_computation.65 | loop fusion | flops 17694720 | bytes 22118400 | tf_op jit(solution)/shard_map/convert_element_type | solution.py:81
  437.6 7.0 %copy.50 = bf16[768,8,360]{2,1,0:T(8,128)(2,1)} copy(bf16[768,8,360]{0,2,1:T(8,128)(2,1)} %bitcast.188) | data formatting | bytes 8847360 | tf_op jit(solution)/shard_map/reshape | solution.py:81
  444.5 108.1 %all_to_all.8 = bf16[768,8,360]{2,1,0:T(8,128)(2,1)S(1)} all-to-all(bf16[768,8,360]{2,1,0:T(8,128)(2,1)} %copy.50), channel_id=1, replica_groups=mesh['parts'=2,'tile'=4,'chan'=4] {'chan'}, dimensions={0} | all-to-all | bytes 8847360 | tf_op jit(solution)/shard_map/all_to_all | solution.py:82
  552.7 3.4 fusion.23
  (33 shorter events, 9.0 us)
Async XLA Ops:
  6.5 8.4 %copy-start.1 = (f32[9,192]{1,0:T(8,128)S(1)}, f32[9,192]{1,0:T(8,128)}, u32[]{:S(2)}) copy-start(f32[9,192]{1,0:T(8,128)} %param.7) | copy-start | bytes 20740
  6.5 8.4 %copy-start.2 = (f32[9,192]{1,0:T(8,128)S(1)}, f32[9,192]{1,0:T(8,128)}, u32[]{:S(2)}) copy-start(f32[9,192]{1,0:T(8,128)} %param.8) | copy-start | bytes 20740
  6.5 268.1 %all-gather.3.cloned.1.call-start = ((), (), s32[]{:S(2)}) async-start(), calls=%async_computation.2 | async-start | bytes 5013504 | tf_op jit(solution)/shard_map/all_gather | solution.py:61
  11.2 9.5 %collective-permute-start.1 = (bf16[192,32,8]{0,2,1:T(8,128)(2,1)S(1)}, bf16[192,32,8]{0,2,1:T(8,128)(2,1)S(1)}, u32[]{:S(2)}, u32[]{:S(2)}) collective-permute-start(bf16[192,32,8]{0,2,1:T(8,128)(2,1)S(1)} %copy.53), channel_id=1, source_target_pairs={{4,0},{8,4},{12,8},{0,12},{5,1},{9,5},{13,9},{1,13},{6,2},{10,6},{... | collective-permute-start | bytes 294920 | tf_op jit(solution)/shard_map/ppermute | solution.py:18
  14.9 4.4 collective-permute-start
  96.7 136.6 %all-to-all-start = ((bf16[192,32,360]{2,0,1:T(8,128)(2,1)}), bf16[192,32,360]{2,0,1:T(8,128)(2,1)}, u32[]{:S(2)}, u32[]{:S(2)}) async-start(bf16[192,32,360]{2,0,1:T(8,128)(2,1)} %copy.39), calls=%async_computation | async-start | bytes 9437184 | tf_op jit(solution)/shard_map/all_to_all | solution.py:57
  101.6 298.0 %all-gather.5.cloned.1.call-start = ((), (), s32[]{:S(2)}) async-start(), calls=%async_computation.3 | async-start | bytes 5013504 | tf_op jit(solution)/shard_map/all_gather | solution.py:67
  255.8 11.7 %copy-start.3 = (f32[768]{0:T(1024)S(1)}, f32[768]{0:T(1024)}, u32[]{:S(2)}) copy-start(f32[768]{0:T(1024)} %param.9) | copy-start | bytes 9220
  399.7 8.8 %copy-start = (bf16[3072,2880]{1,0:T(8,128)(2,1)S(1)}, bf16[3072,2880]{1,0:T(8,128)(2,1)}, u32[]{:S(2)}) copy-start(bf16[3072,2880]{1,0:T(8,128)(2,1)} %copy.41) | copy-start | bytes 53084164
  399.7 10.8 %copy-start.4 = (bf16[768,3072]{0,1:T(8,128)(2,1)S(1)}, bf16[768,3072]{0,1:T(8,128)(2,1)}, u32[]{:S(2)}) copy-start(bf16[768,3072]{0,1:T(8,128)(2,1)} %all-gather.5.cloned.1.call-done) | copy-start | bytes 14155780
  437.6 115.1 %slice-start = ((s8[4718592]{0:T(1024)(128)(4,1)}), s8[524288]{0:T(1024)(128)(4,1)S(1)}, s32[]{:S(2)}) async-start(s8[4718592]{0:T(1024)(128)(4,1)} %bitcast.181), calls=%async_computation.4 | async-start | bytes 1048576
  444.5 108.1 %slice-start.1 = ((s8[4718592]{0:T(1024)(128)(4,1)}), s8[4194304]{0:T(1024)(128)(4,1)S(1)}, s32[]{:S(2)}) async-start(s8[4718592]{0:T(1024)(128)(4,1)} %bitcast.181), calls=%async_computation.5 | async-start | bytes 8388608
Sparse Core Ops, SparseCore 0:
  9.7 56.0 all-gather.2
  104.8 103.3 all-gather.4
where the time goes:
time: 572 us; the launch traced here: 563 us
  waiting for transfers between devices  136 us (24%)
  matrix products  128 us (22%)
  blocking collectives  108 us (19%)
  other arithmetic  105 us (18%)
  local copies, waits for them, and re-layouts  63.8 us (11%)
  between operations  14 us (2%)
  starting transfers between devices  7.74 us (1%)
    all_to_all x1, waiting for transfers between devices, on_device(): lax.all_to_all(spatial, 'chan', split_axis=1, concat_axis=0, tiled=True)  131 us
    all_to_all x1, blocking collectives, on_device(): lax.all_to_all(update_cells, 'chan', split_axis=0, concat_axis=1, tiled=T...  108 us
    dot_general x1, matrix products, on_device(): lax.dot_general(lax.all_gather(up_weight, ('tile', 'chan'), axis=1, tiled...  103 us
    add x1, other arithmetic, on_device(): lon_sum + lon_taps[kernel_tap_index][:, None, None] * sliding_window  36.4 us
    convert_element_type x1, other arithmetic, on_device(): spatial = latitude_sum.astype(jnp.bfloat16)  34.3 us
    dot_general x4, matrix products, on_device(): jnp.einsum('dts,tsc->dc', down_groups[:, :, group, :], hidden_groups[:, g...  25.5 us
    convert_element_type x1, local copies, waits for them, and re-layouts, on_device(): hidden = jax.nn.gelu(expanded, approximate=False).astype(jnp.bfloat16)  22.1 us
    convert_element_type x2, local copies, waits for them, and re-layouts, layer_norm(): as_float = values.astype(jnp.float32)  20.6 us
  transfers between devices with their start and end apart: 5, of which 2 were waited for; matrix products, arithmetic and copies ran while one was open for 44% of the time, Pallas kernels for 0%

commit v1 on v0

--- a/solution.py
+++ b/solution.py
@@ -54,7 +54,9 @@
     group_count = lax.axis_size("chan")
     width_all = chan_count * group_count
     shard_width = up_weight.shape[1]
-    by_cell = lax.all_to_all(spatial, "chan", split_axis=1, concat_axis=0, tiled=True)
+    shards = jnp.split(spatial, lax.axis_size("chan"), axis=1)
+    received = lax.all_to_all(jnp.stack(shards), "chan", 0, 0)
+    by_cell = jnp.concatenate(received, axis=0)
     cell_count = by_cell.shape[1] * by_cell.shape[2]
     normed = layer_norm(by_cell.reshape(width_all, cell_count), norm_gain)
     expanded = lax.dot_general(

time: 572 us -> 544 us (0.951)
  local copies, waits for them, and re-layouts: 63.8 us -> 49.1 us
  starting transfers between devices: 7.74 us -> 21.1 us
  waiting for transfers between devices: 136 us -> 123 us
  matrix products: 128 us -> 118 us
    all_gather x1, starting transfers between devices: 0.3 us -> 13.7 us  [on_device(): down_all = lax.all_gather(down_weight, ('tile', 'chan'), axis=1, tiled=True)]
    all_to_all x1, waiting for transfers between devices: 131 us -> 118 us  [on_device(): received = lax.all_to_all(jnp.stack(shards), 'chan', 0, 0)]
    convert_element_type x2 -> x1, local copies, waits for them, and re-layouts: 20.6 us -> 9.67 us  [layer_norm(): as_float = values.astype(jnp.float32)]
    dot_general x1, matrix products: 103 us -> 92.1 us  [on_device(): lax.dot_general(lax.all_gather(up_weight, ('tile', 'chan'), axis=1, tiled...]
  transfers between devices with their start and end apart: 5 -> 5, of which waited for: 2 -> 2; matrix products, arithmetic and copies ran while one was open for 44% -> 41% of each run, Pallas kernels for 0% -> 0%
where the time goes in v1:
time: 544 us; the launch traced here: 535 us
  waiting for transfers between devices  123 us (23%)
  matrix products  118 us (22%)
  blocking collectives  108 us (20%)
  other arithmetic  102 us (19%)
  local copies, waits for them, and re-layouts  49.1 us (9%)
  starting transfers between devices  21.1 us (4%)
  between operations  14 us (3%)
    all_to_all x1, waiting for transfers between devices, on_device(): received = lax.all_to_all(jnp.stack(shards), 'chan', 0, 0)  118 us
    all_to_all x1, blocking collectives, on_device(): lax.all_to_all(update_cells, 'chan', split_axis=0, concat_axis=1, tiled=T...  108 us
    dot_general x1, matrix products, on_device(): lax.dot_general(lax.all_gather(up_weight, ('tile', 'chan'), axis=1, tiled...  92.1 us
    add x1, other arithmetic, on_device(): lon_sum + lon_taps[kernel_tap_index][:, None, None] * sliding_window  37 us
    convert_element_type x1, other arithmetic, on_device(): spatial = latitude_sum.astype(jnp.bfloat16)  34.8 us
    dot_general x4, matrix products, on_device(): jnp.einsum('dts,tsc->dc', down_groups[:, :, group, :], hidden_groups[:, g...  25.4 us
    convert_element_type x1, local copies, waits for them, and re-layouts, on_device(): hidden = jax.nn.gelu(expanded, approximate=False).astype(jnp.bfloat16)  21.9 us
    all_gather x1, starting transfers between devices, on_device(): down_all = lax.all_gather(down_weight, ('tile', 'chan'), axis=1, tiled=True)  13.7 us
  transfers between devices with their start and end apart: 5, of which 2 were waited for; matrix products, arithmetic and copies ran while one was open for 41% of the time, Pallas kernels for 0%

profile of v1, /device:TPU:0, one launch (start us, length us, event | category | flops | bytes accessed | tf_op | source)
XLA Modules:
  0.0 535.0 jit_solution(12470610121679659133)
XLA Ops:
  7.3 2.6 fusion.55
  11.2 2.4 collective-permute-start.1
  15.0 4.3 collective-permute-done
  22.0 37.0 %fusion.22 = f32[192,32,360]{2,1,0:T(8,128)} fusion(bf16[192,32,360]{2,1,0:T(8,128)(2,1)} %param.6, bf16[192,32,8]{2,1,0:T(8,128)(2,1)S(1)} %copy.36, bf16[192,32,8]{2,1,0:T(8,128)(2,1)S(1)} %copy.34, f32[192]{0:T(256)S(1)} %bitcast.202, f32[192]{0:T(256)S(1)} %bitcast.203, f32[192]{0:T(256)S(1)} %bitcast.196, f32[192]{0:T(256)S(1)} %bitcast.197, ...), kind=kLoop, calls=%fused_computation.38 | loop fusion | flops 110592000 | bytes 13474560 | tf_op jit(solution)/shard_map/add | solution.py:40
  59.0 34.8 %fusion.33 = bf16[192,32,360]{2,1,0:T(8,128)(2,1)S(1)} fusion(f32[192,32,360]{2,1,0:T(8,128)} %fusion.22, f32[192]{0:T(256)S(1)} %bitcast.193, f32[192]{0:T(256)S(1)} %bitcast.194, f32[192]{0:T(256)S(1)} %bitcast.187, f32[192]{0:T(256)S(1)} %bitcast.188, f32[192]{0:T(256)S(1)} %bitcast.189, f32[192]{0:T(256)S(1)} %bitcast.190, f32[192]{0:T(256)S(1)} %bitcast.191, ...), kind=kLoop, calls=%fused_computation.49 | loop fusion | flops 39813120 | bytes 13277952 | tf_op jit(solution)/shard_map/convert_element_type | solution.py:53
  94.2 2.8 pad_maximum_fusion.2
  97.0 4.9 all-to-all-start
  101.9 13.7 %all-gather.5.cloned.1.call-start = ((), (), s32[]{:S(2)}) async-start(), calls=%async_computation.3 | async-start | bytes 5013504 | tf_op jit(solution)/shard_map/all_gather | solution.py:69
  115.7 117.9 %all-to-all-done = bf16[4,192,8,360]{3,2,1,0:T(8,128)(2,1)} async-done(((bf16[4,192,8,360]{3,2,1,0:T(8,128)(2,1)}), bf16[4,192,8,360]{3,2,1,0:T(8,128)(2,1)}, u32[]{:S(2)}, u32[]{:S(2)}) %all-to-all-start) | async-done | bytes 4423712 | tf_op jit(solution)/shard_map/all_to_all | solution.py:58
  233.6 3.2 convert_reduce_fusion
  236.9 3.7 multiply_reduce_fusion
  240.7 9.7 %reshape.65 = f32[768,2880]{1,0:T(8,128)} reshape(bf16[4,192,8,360]{3,2,1,0:T(8,128)(2,1)} %all-to-all-done) | data formatting | bytes 13271040 | tf_op jit(solution)/shard_map/convert_element_type | solution.py:24
  250.3 7.1 %multiply_convert_fusion.1.clone.4 = bf16[768,2880]{1,0:T(8,128)(2,1)} fusion(f32[768,2880]{1,0:T(8,128)} %reshape.65, f32[768]{0:T(1024)S(1)} %copy-done.3, f32[2880]{0:T(1024)S(1)} %rsqrt.11, f32[2880]{0:T(1024)S(1)} %div.9), kind=kLoop, calls=%fused_computation.59.clone.clone.clone.clone.1 | loop fusion | flops 8847360 | bytes 13297152 | tf_op jit(solution)/shard_map/convert_element_type | solution.py:68
  257.4 92.1 %fusion.2 = bf16[3072,2880]{0,1:T(8,128)(2,1)} fusion(bf16[768,3072]{0,1:T(8,128)(2,1)} %all-gather.3.cloned.1.call-done, bf16[768,2880]{1,0:T(8,128)(2,1)} %multiply_convert_fusion.1.clone.4), kind=kOutput, calls=%fused_computation.3 | convolution fusion | flops 14164623360 | bytes 26836992 | tf_op jit(solution)/shard_map/dot_general | solution.py:62
  349.5 21.9 %copy.37 = bf16[3072,2880]{1,0:T(8,128)(2,1)} copy(bf16[3072,2880]{0,1:T(8,128)(2,1)} %fusion.2) | data formatting | bytes 35389440 | tf_op jit(solution)/shard_map/convert_element_type | solution.py:68
  371.4 8.7 %fusion.53 = bf16[768,2880]{0,1:T(8,128)(2,1)} fusion(bf16[4,4,192,2880]{3,2,1,0:T(8,128)(2,1)} %bitcast.181, bf16[768,4,4,192]{0,3,2,1:T(8,128)(2,1)} %bitcast.204), kind=kOutput, calls=%fused_computation.93 | convolution fusion | flops 3399598080 | bytes 10125312 | tf_op jit(solution)/shard_map/dts,tsc->dc/dot_general | solution.py:75
  380.3 1.9 copy-done.4
  382.2 5.5 %fusion.52 = bf16[768,2880]{0,1:T(8,128)(2,1)} fusion(bf16[4,4,192,2880]{3,2,1,0:T(8,128)(2,1)S(1)} %bitcast.182, bf16[768,4,4,192]{0,3,2,1:T(8,128)(2,1)S(1)} %bitcast.205), kind=kOutput, calls=%fused_computation.92 | convolution fusion | flops 3399598080 | bytes 10125312 | tf_op jit(solution)/shard_map/dts,tsc->dc/dot_general | solution.py:75
  387.7 5.6 %fusion.51 = bf16[768,2880]{0,1:T(8,128)(2,1)} fusion(bf16[4,4,192,2880]{3,2,1,0:T(8,128)(2,1)S(1)} %bitcast.183, bf16[768,4,4,192]{0,3,2,1:T(8,128)(2,1)S(1)} %bitcast.206), kind=kOutput, calls=%fused_computation.91 | convolution fusion | flops 3399598080 | bytes 10125312 | tf_op jit(solution)/shard_map/dts,tsc->dc/dot_general | solution.py:75
  393.2 5.7 %fusion.54 = bf16[768,2880]{0,1:T(8,128)(2,1)} fusion(bf16[4,4,192,2880]{3,2,1,0:T(8,128)(2,1)S(1)} %bitcast.184, bf16[768,4,4,192]{0,3,2,1:T(8,128)(2,1)S(1)} %bitcast.207), kind=kOutput, calls=%fused_computation.94 | convolution fusion | flops 3399598080 | bytes 10125312 | tf_op jit(solution)/shard_map/dts,tsc->dc/dot_general | solution.py:75
  398.9 10.3 %add_convert_fusion = bf16[768,2880]{0,1:T(8,128)(2,1)} fusion(bf16[768,2880]{0,1:T(8,128)(2,1)} %fusion.54, bf16[768,2880]{0,1:T(8,128)(2,1)} %fusion.53, bf16[768,2880]{0,1:T(8,128)(2,1)} %fusion.52, bf16[768,2880]{0,1:T(8,128)(2,1)} %fusion.51), kind=kLoop, calls=%fused_computation.64 | loop fusion | flops 17694720 | bytes 22118400 | tf_op jit(solution)/shard_map/convert_element_type | solution.py:83
  409.3 7.0 %copy.46 = bf16[768,8,360]{2,1,0:T(8,128)(2,1)} copy(bf16[768,8,360]{0,2,1:T(8,128)(2,1)} %bitcast.185) | data formatting | bytes 8847360 | tf_op jit(solution)/shard_map/reshape | solution.py:83
  416.2 108.1 %all_to_all.14 = bf16[768,8,360]{2,1,0:T(8,128)(2,1)S(1)} all-to-all(bf16[768,8,360]{2,1,0:T(8,128)(2,1)} %copy.46), channel_id=1, replica_groups=mesh['parts'=2,'tile'=4,'chan'=4] {'chan'}, dimensions={0} | all-to-all | bytes 8847360 | tf_op jit(solution)/shard_map/all_to_all | solution.py:84
  524.3 3.4 fusion.23
  (32 shorter events, 6.8 us)
Async XLA Ops:
  6.5 8.4 %copy-start.1 = (f32[9,192]{1,0:T(8,128)S(1)}, f32[9,192]{1,0:T(8,128)}, u32[]{:S(2)}) copy-start(f32[9,192]{1,0:T(8,128)} %param.7) | copy-start | bytes 20740
  6.5 8.4 %copy-start.2 = (f32[9,192]{1,0:T(8,128)S(1)}, f32[9,192]{1,0:T(8,128)}, u32[]{:S(2)}) copy-start(f32[9,192]{1,0:T(8,128)} %param.8) | copy-start | bytes 20740
  6.5 250.9 %all-gather.3.cloned.1.call-start = ((), (), s32[]{:S(2)}) async-start(), calls=%async_computation.2 | async-start | bytes 5013504 | tf_op jit(solution)/shard_map/all_gather | solution.py:63
  11.2 9.5 %collective-permute-start.1 = (bf16[192,32,8]{0,2,1:T(8,128)(2,1)S(1)}, bf16[192,32,8]{0,2,1:T(8,128)(2,1)S(1)}, u32[]{:S(2)}, u32[]{:S(2)}) collective-permute-start(bf16[192,32,8]{0,2,1:T(8,128)(2,1)S(1)} %copy.49), channel_id=1, source_target_pairs={{4,0},{8,4},{12,8},{0,12},{5,1},{9,5},{13,9},{1,13},{6,2},{10,6},{... | collective-permute-start | bytes 294920 | tf_op jit(solution)/shard_map/ppermute | solution.py:18
  14.9 4.4 collective-permute-start
  97.0 136.6 %all-to-all-start = ((bf16[4,192,8,360]{3,2,1,0:T(8,128)(2,1)}), bf16[4,192,8,360]{3,2,1,0:T(8,128)(2,1)}, u32[]{:S(2)}, u32[]{:S(2)}) async-start(bf16[4,192,8,360]{3,2,1,0:T(8,128)(2,1)} %pad_maximum_fusion.2), calls=%async_computation | async-start | bytes 9437184 | tf_op jit(solution)/shard_map/all_to_all | solution.py:58
  101.9 269.5 %all-gather.5.cloned.1.call-start = ((), (), s32[]{:S(2)}) async-start(), calls=%async_computation.3 | async-start | bytes 5013504 | tf_op jit(solution)/shard_map/all_gather | solution.py:69
  236.8 13.6 %copy-start.3 = (f32[768]{0:T(1024)S(1)}, f32[768]{0:T(1024)}, u32[]{:S(2)}) copy-start(f32[768]{0:T(1024)} %param.9) | copy-start | bytes 9220
  371.4 8.8 %copy-start = (bf16[3072,2880]{1,0:T(8,128)(2,1)S(1)}, bf16[3072,2880]{1,0:T(8,128)(2,1)}, u32[]{:S(2)}) copy-start(bf16[3072,2880]{1,0:T(8,128)(2,1)} %copy.37) | copy-start | bytes 53084164
  371.4 10.8 %copy-start.4 = (bf16[768,3072]{0,1:T(8,128)(2,1)S(1)}, bf16[768,3072]{0,1:T(8,128)(2,1)}, u32[]{:S(2)}) copy-start(bf16[768,3072]{0,1:T(8,128)(2,1)} %all-gather.5.cloned.1.call-done) | copy-start | bytes 14155780
  409.3 115.1 %slice-start = ((s8[4718592]{0:T(1024)(128)(4,1)}), s8[524288]{0:T(1024)(128)(4,1)S(1)}, s32[]{:S(2)}) async-start(s8[4718592]{0:T(1024)(128)(4,1)} %bitcast.178), calls=%async_computation.4 | async-start | bytes 1048576
  416.2 108.1 %slice-start.1 = ((s8[4718592]{0:T(1024)(128)(4,1)}), s8[4194304]{0:T(1024)(128)(4,1)S(1)}, s32[]{:S(2)}) async-start(s8[4718592]{0:T(1024)(128)(4,1)} %bitcast.178), calls=%async_computation.5 | async-start | bytes 8388608
Sparse Core Ops, SparseCore 0:
  9.7 56.0 all-gather.2
  115.8 114.8 all-gather.4
